TPU v7x, 32 devices: a whole 2x2x4 slice. The times are simulated.
32 devices in a mesh: grp: 4 (over x, core), env: 8 (over z, y).
Axes of the slice: x: 2, y: 2, z: 4, core: 2. Of those that a mesh axis runs over, the one named last changes fastest.
Arguments:
- wavefunction: bfloat16 [8192, 1024], P('grp', 'env'), may hold values from -6 to 6
- left_tiles: bfloat16 [512, 128, 128], P(('grp', 'env')), may hold values from -0.5 to 0.5
- right_tiles: bfloat16 [26, 1024, 128], P(None, 'env'), may hold values from -0.5 to 0.5
- term_source: int32 [512], P('grp'), may hold values from 0 to 63
- term_target: int32 [512], P('grp'), may hold values from 0 to 63
- right_index: int32 [512], P('grp'), may hold values from 0 to 25
- term_sector: int32 [512, 1], P('grp'), may hold values from 0 to 31; in each aligned block of 16 rows (0 to 15, 16 to 31, ...) at most 4 rows name the same one
- column_sector: int32 [8], replicated, may hold values from 0 to 31
Outputs:
- applied: bfloat16 [8192, 1024], P('grp', 'env')
Inputs may be any that keep to these rules, and one draw needn't show every extreme that they name: `term_sector`: within each aligned block of 16 terms (the terms of one device) no sector appears more than 4 times, and every sector appears somewhere.
All inputs are finite; a program needn't handle non-finite values.
Results may differ from a plain program's by a relative error of at most 0.009.
Values may be sent and summed in bfloat16 or wider, within the bound.
A program may use at most 64 MiB of HBM per device.

v0:
```python
import jax
import jax.numpy as jnp
from jax import lax
from jax.sharding import PartitionSpec as P

MAXS = 4


def contribute(
    running, left_pick, source_rows, target_rows, right_rows, kept_mask, blocks, right_tiles
):
    source_blocks = blocks[source_rows]
    block_product = jnp.einsum(
        "kab,kbc->kac", left_pick, source_blocks, preferred_element_type=jnp.float32
    ).astype(jnp.bfloat16)
    term_image = jnp.einsum(
        "kac,kcd->kad", block_product, right_tiles[right_rows], preferred_element_type=jnp.float32
    )
    term_image = term_image * kept_mask[:, None, None]
    return running.at[target_rows].add(term_image)


def shards(
    wavefunction,
    left_tiles,
    right_tiles,
    term_source,
    term_target,
    right_index,
    term_sector,
    column_sector,
):
    tile_size = left_tiles.shape[1]
    env_count = lax.axis_size("env")
    env_place = lax.axis_index("env")
    sectors = term_sector[:, 0]
    my_sector = column_sector[env_place]
    gathered = lax.all_gather(wavefunction, "grp", axis=0, tiled=True)
    block_count = gathered.shape[0] // tile_size
    blocks = gathered.reshape(block_count, tile_size, tile_size)
    running = jnp.zeros((block_count, tile_size, tile_size), jnp.float32)
    tiles_dev = left_tiles.shape[0]
    sector_grid = sectors.reshape(env_count, tiles_dev)
    own_sectors = sector_grid[env_place]
    outgoing_miss = (own_sectors[None, :] != column_sector[:, None]).astype(jnp.int32)
    outgoing_pick = jnp.argsort(outgoing_miss, axis=1, stable=True)[:, :MAXS]
    outgoing = left_tiles[outgoing_pick]
    incoming = lax.all_to_all(outgoing, "env", split_axis=0, concat_axis=0, tiled=True)
    incoming_miss = (sector_grid != my_sector).astype(jnp.int32)
    incoming_pick = jnp.argsort(incoming_miss, axis=1, stable=True)[:, :MAXS]
    chosen = (jnp.arange(env_count, dtype=jnp.int32)[:, None] * tiles_dev + incoming_pick).reshape(
        -1
    )
    kept_mask = (
        (1 - jnp.take_along_axis(incoming_miss, incoming_pick, axis=1))
        .reshape(-1)
        .astype(jnp.float32)
    )
    running = contribute(
        running,
        incoming.reshape(-1, tile_size, tile_size),
        term_source[chosen],
        term_target[chosen],
        right_index[chosen],
        kept_mask,
        blocks,
        right_tiles,
    )
    summed = lax.psum_scatter(
        running.reshape(block_count * tile_size, tile_size).astype(jnp.bfloat16),
        "grp",
        scatter_dimension=0,
        tiled=True,
    )
    return summed


def solution(mesh):
    placed = (
        P("grp", "env"),
        P(("grp", "env"), None, None),
        P(None, "env", None),
        P("grp"),
        P("grp"),
        P("grp"),
        P("grp", None),
        P(),
    )
    return jax.shard_map(
        shards, mesh=mesh, in_specs=placed, out_specs=P("grp", "env"), check_vma=False
    )
```

profile of v0, /device:TPU:0, one launch (start us, length us, event | category | flops | bytes accessed | tf_op | source)
XLA Modules:
  0.0 99.9 jit_solution(12645802424836200396)
XLA Ops:
  6.5 0.0 copy-start
  6.5 0.0 all-gather.2.cloned.1.call-start
  6.5 0.7 all-gather.2.cloned.1.call-update
  7.3 0.5 broadcast.147
  7.8 1.3 %reduce.3 = s32[128]{0:T(128)S(1)} reduce(s32[128,1]{0,1:T(1,128)} %param.14, s32[]{:T(128)} %broadcast.147), dimensions={1}, to_apply=%param.14.reduce_sub_computation.3 | reduce | bytes 1028 | tf_op args[6]
  9.1 0.1 reshape_squeeze.3
  9.2 0.7 compare_convert_fusion
  9.9 0.7 sort.32
  10.6 0.1 copy.13
  10.7 0.1 reshape.126
  10.8 0.0 copy-start.5
  10.8 2.7 %gather_fusion.1 = bf16[32,128,128]{2,1,0:T(8,128)(2,1)} fusion(bf16[16,128,128]{2,1,0:T(8,128)(2,1)} %param.9, s32[1024]{0:T(1024)S(1)} %pad_clamp_fusion.2), kind=kCustom, calls=%fused_computation.1 | custom fusion | bytes 2097280 | tf_op jit(solution)/shard_map/gather | solution.py:47
  13.5 7.3 %all-to-all-start = ((bf16[8,4,128,128]{3,2,1,0:T(8,128)(2,1)}), bf16[8,4,128,128]{3,2,1,0:T(8,128)(2,1)S(1)}, u32[]{:S(2)}, u32[]{:S(2)}) async-start(bf16[8,4,128,128]{3,2,1,0:T(8,128)(2,1)} %bitcast.5), calls=%async_computation | async-start | bytes 2097152 | tf_op jit(solution)/shard_map/all_to_all | solution.py:48
  20.8 0.0 reduce-scatter.2.cloned.1.call-start
  20.9 0.0 copy-done.5
  20.9 0.6 dynamic_slice.6
  21.5 0.6 compare_convert_fusion.1
  22.1 0.1 copy.11
  22.2 0.7 sort.31
  22.9 0.1 copy.14
  23.0 0.1 reshape.164
  23.1 0.0 copy-start.1
  23.1 0.0 copy-start.3
  23.1 0.7 gather_fusion.6
  23.8 0.1 reshape.167
  23.9 0.1 copy.15
  24.0 0.1 copy.16
  24.0 0.1 convert_element_type.29
  24.1 0.1 copy.12
  24.2 0.1 reshape.112
  24.3 0.0 copy-done.1
  24.3 0.7 gather_fusion.4
  25.0 0.0 copy-done.2
  25.0 0.7 gather_fusion.2
  25.7 0.0 copy-done.3
  25.7 0.7 gather_fusion
  26.5 0.0 copy-done
  26.5 1.7 %gather_fusion.5 = bf16[32,128,128]{2,1,0:T(8,128)(2,1)} fusion(bf16[26,128,128]{2,1,0:T(8,128)(2,1)S(1)} %copy-done, s32[1024]{0:T(1024)S(1)} %pad_clamp_fusion), kind=kCustom, calls=%fused_computation.5 | custom fusion | bytes 2097280 | tf_op jit(solution)/shard_map/gather | solution.py:17
  28.2 6.1 %all-gather.2.cloned.1.call-done = bf16[8192,128]{1,0:T(8,128)(2,1)} async-done(((bf16[2048,128]{1,0:T(8,128)(2,1)}), bf16[8192,128]{1,0:T(8,128)(2,1)}) %all-gather.2.cloned.1.call-update) | async-done | bytes 2097168 | tf_op jit(solution)/shard_map/all_gather | solution.py:38
  34.2 3.3 %gather_fusion.3 = bf16[32,128,128]{2,1,0:T(8,128)(2,1)} fusion(bf16[64,128,128]{2,1,0:T(8,128)(2,1)} %bitcast.31, s32[1024]{0:T(1024)S(1)} %pad_clamp_fusion.1), kind=kCustom, calls=%fused_computation.3 | custom fusion | bytes 2097280 | tf_op jit(solution)/shard_map/gather | solution.py:12
  37.5 9.1 %all-to-all-done = bf16[8,4,128,128]{3,2,1,0:T(8,128)(2,1)S(1)} async-done(((bf16[8,4,128,128]{3,2,1,0:T(8,128)(2,1)}), bf16[8,4,128,128]{3,2,1,0:T(8,128)(2,1)S(1)}, u32[]{:S(2)}, u32[]{:S(2)}) %all-to-all-start) | async-done | bytes 1048608 | tf_op jit(solution)/shard_map/all_to_all | solution.py:48
  46.6 1.0 copy-done.4
  47.6 2.6 %convolution_multiply_fusion = f32[32,128,128]{2,1,0:T(8,128)S(1)} fusion(bf16[32,128,128]{2,1,0:T(8,128)(2,1)} %gather_fusion.5, bf16[32,128,128]{2,1,0:T(8,128)(2,1)} %bitcast.30, bf16[32,128,128]{2,1,0:T(8,128)(2,1)} %gather_fusion.3, f32[32]{0:T(128)S(1)} %convert_element_type.29), kind=kOutput, calls=%fused_computation.8 | convolution fusion | flops 269484032 | bytes 5243008 | tf_op jit(solution)/shard_map/kac,kcd->kad/dot_general | solution.py:16
  50.2 2.4 %broadcast_in_dim.8 = f32[64,128,128]{2,1,0:T(8,128)} broadcast(f32[]{:T(128)} %constant.11.clone.1), dimensions={} | broadcast | bytes 4194308 | tf_op jit(solution)/shard_map/broadcast_in_dim | solution.py:41
  52.6 6.1 %scatter_fusion = f32[64,128,128]{2,1,0:T(8,128)} fusion(f32[64,128,128]{2,1,0:T(8,128)} %broadcast_in_dim.8, s32[32]{0:T(128)S(1)} %fusion.1, f32[32,128,128]{2,1,0:T(8,128)S(1)} %convolution_multiply_fusion), kind=kCustom, calls=%fused_computation.7 | custom fusion | flops 524288 | bytes 6291584 | tf_op jit(solution)/shard_map/scatter-add | solution.py:20
  58.7 3.9 %convert_element_type.30 = bf16[64,128,128]{2,1,0:T(8,128)(2,1)} convert(f32[64,128,128]{2,1,0:T(8,128)} %scatter_fusion) | non-fusion elementwise | flops 1048576 | bytes 6291456 | tf_op jit(solution)/shard_map/convert_element_type | solution.py:70
  62.6 0.0 reduce-scatter.2.cloned.1.call-update
  62.7 30.4 %reduce-scatter.2.cloned.1.call-done = bf16[2048,128]{1,0:T(8,128)(2,1)} async-done(((bf16[8192,128]{1,0:T(8,128)(2,1)}), bf16[2048,128]{1,0:T(8,128)(2,1)}) %reduce-scatter.2.cloned.1.call-update) | async-done | bytes 524304 | tf_op jit(solution)/shard_map/reduce_scatter | solution.py:69
  (17 shorter events, 0.1 us)
Async XLA Ops:
  6.5 19.9 %copy-start = (bf16[26,128,128]{2,1,0:T(8,128)(2,1)S(1)}, bf16[26,128,128]{2,1,0:T(8,128)(2,1)}, u32[]{:S(2)}) copy-start(bf16[26,128,128]{2,1,0:T(8,128)(2,1)} %param.10) | copy-start | bytes 2555908
  6.5 27.7 %all-gather.2.cloned.1.call-start = ((), (), s32[]{:S(2)}) async-start(), calls=%async_computation.2 | async-start | bytes 2621440 | tf_op jit(solution)/shard_map/all_gather | solution.py:38
  10.8 10.1 %copy-start.5 = (s32[8]{0:T(128)S(1)}, s32[8]{0:T(128)}, u32[]{:S(2)}) copy-start(s32[8]{0:T(128)} %param.15) | copy-start | bytes 100
  13.5 33.1 %all-to-all-start = ((bf16[8,4,128,128]{3,2,1,0:T(8,128)(2,1)}), bf16[8,4,128,128]{3,2,1,0:T(8,128)(2,1)S(1)}, u32[]{:S(2)}, u32[]{:S(2)}) async-start(bf16[8,4,128,128]{3,2,1,0:T(8,128)(2,1)} %bitcast.5), calls=%async_computation | async-start | bytes 2097152 | tf_op jit(solution)/shard_map/all_to_all | solution.py:48
  20.8 72.2 %reduce-scatter.2.cloned.1.call-start = ((), (), s32[]{:S(2)}) async-start(), calls=%async_computation.3 | async-start | bytes 2621440 | tf_op jit(solution)/shard_map/reduce_scatter | solution.py:69
  23.1 1.2 %copy-start.1 = (s32[128]{0:T(128)S(1)}, s32[128]{0:T(128)}, u32[]{:S(2)}) copy-start(s32[128]{0:T(128)} %param.13) | copy-start | bytes 1540
  23.1 1.9 %copy-start.2 = (s32[128]{0:T(128)S(1)}, s32[128]{0:T(128)}, u32[]{:S(2)}) copy-start(s32[128]{0:T(128)} %param.11) | copy-start | bytes 1540
  23.1 2.6 %copy-start.3 = (s32[128]{0:T(128)S(1)}, s32[128]{0:T(128)}, u32[]{:S(2)}) copy-start(s32[128]{0:T(128)} %param.12) | copy-start | bytes 1540
  46.6 1.0 copy-start.4
Sparse Core Ops, SparseCore 0:
  8.9 25.2 all-gather.1
  62.8 30.2 reduce-scatter.1
where the time goes:
time: 100 us; the launch traced here: 99.9 us
  waiting for transfers between devices  46.3 us (46%)
  local copies, waits for them, and re-layouts  15.9 us (16%)
  other arithmetic  14.2 us (14%)
  between operations  13.5 us (14%)
  starting transfers between devices  7.35 us (7%)
  matrix products  2.57 us (3%)
    reduce_scatter x1, waiting for transfers between devices, shards(): lax.psum_scatter(running.reshape(block_count * tile_size, tile_size).asty...  30.4 us
    all_to_all x1, waiting for transfers between devices, shards(): lax.all_to_all(outgoing, 'env', split_axis=0, concat_axis=0, tiled=True)  9.13 us
    all_to_all x1, starting transfers between devices, shards(): lax.all_to_all(outgoing, 'env', split_axis=0, concat_axis=0, tiled=True)  7.31 us
    scatter-add x1, other arithmetic, contribute(): return running.at[target_rows].add(term_image)  6.13 us
    all_gather x1, waiting for transfers between devices, shards(): gathered = lax.all_gather(wavefunction, 'grp', axis=0, tiled=True)  6.05 us
    convert_element_type x1, other arithmetic, shards(): running.reshape(block_count * tile_size, tile_size).astype(jnp.bfloat16)  3.9 us
    gather x1, local copies, waits for them, and re-layouts, contribute(): source_blocks = blocks[source_rows]  3.25 us
    gather x1, local copies, waits for them, and re-layouts, shards(): outgoing = left_tiles[outgoing_pick]  2.7 us
  transfers between devices with their start and end apart: 3, of which 3 were waited for; matrix products, arithmetic and copies ran while one was open for 17% of the time, Pallas kernels for 0%

commit v1 on v0

--- a/solution.py
+++ b/solution.py
@@ -35,7 +35,12 @@
     env_place = lax.axis_index("env")
     sectors = term_sector[:, 0]
     my_sector = column_sector[env_place]
-    gathered = lax.all_gather(wavefunction, "grp", axis=0, tiled=True)
+    ring = [wavefunction]
+    for hop in range(3):
+        ring.append(lax.ppermute(ring[-1], "grp", [(dev, (dev + 1) % 4) for dev in range(4)]))
+    gathered = jnp.roll(
+        jnp.concatenate(ring[::-1], axis=0), (lax.axis_index("grp") + 1) * ring[0].shape[0], axis=0
+    )
     block_count = gathered.shape[0] // tile_size
     blocks = gathered.reshape(block_count, tile_size, tile_size)
     running = jnp.zeros((block_count, tile_size, tile_size), jnp.float32)

time: 100 us -> 99.7 us (level)
  local copies, waits for them, and re-layouts: 15.9 us -> 14.1 us
  starting transfers between devices: 7.35 us -> 8.84 us
    ppermute x0 -> x3, waiting for transfers between devices: none -> 11.7 us  [shards(): lax.ppermute(ring[-1], 'grp', [(dev, (dev + 1) % 4) for dev in range(4)])]
    all_gather x1 -> x0, waiting for transfers between devices: 6.05 us -> none  [shards(): gathered = lax.all_gather(wavefunction, 'grp', axis=0, tiled=True)]
    all_to_all x1, waiting for transfers between devices: 9.13 us -> 4.58 us  [shards(): lax.all_to_all(outgoing, 'env', split_axis=0, concat_axis=0, tiled=True)]
    ppermute x0 -> x3, starting transfers between devices: none -> 1.85 us  [shards(): lax.ppermute(ring[-1], 'grp', [(dev, (dev + 1) % 4) for dev in range(4)])]
    gather x1, local copies, waits for them, and re-layouts: 3.25 us -> 1.66 us  [contribute(): source_blocks = blocks[source_rows]]
  transfers between devices with their start and end apart: 3 -> 5, of which waited for: 3 -> 4; matrix products, arithmetic and copies ran while one was open for 17% -> 16% of each run, Pallas kernels for 0% -> 0%
where the time goes in v1:
time: 99.7 us; the launch traced here: 99.3 us
  waiting for transfers between devices  46.1 us (46%)
  other arithmetic  14.2 us (14%)
  local copies, waits for them, and re-layouts  14.1 us (14%)
  between operations  13.6 us (14%)
  starting transfers between devices  8.84 us (9%)
  matrix products  2.57 us (3%)
    reduce_scatter x1, waiting for transfers between devices, shards(): lax.psum_scatter(running.reshape(block_count * tile_size, tile_size).asty...  29.8 us
    ppermute x3, waiting for transfers between devices, shards(): lax.ppermute(ring[-1], 'grp', [(dev, (dev + 1) % 4) for dev in range(4)])  11.7 us
    all_to_all x1, starting transfers between devices, shards(): lax.all_to_all(outgoing, 'env', split_axis=0, concat_axis=0, tiled=True)  6.95 us
    scatter-add x1, other arithmetic, contribute(): return running.at[target_rows].add(term_image)  6.13 us
    all_to_all x1, waiting for transfers between devices, shards(): lax.all_to_all(outgoing, 'env', split_axis=0, concat_axis=0, tiled=True)  4.58 us
    convert_element_type x1, other arithmetic, shards(): running.reshape(block_count * tile_size, tile_size).astype(jnp.bfloat16)  3.9 us
    gather x1, local copies, waits for them, and re-layouts, shards(): outgoing = left_tiles[outgoing_pick]  2.72 us
    dot_general x1, matrix products, contribute(): jnp.einsum('kac,kcd->kad', block_product, right_tiles[right_rows], prefer...  2.57 us
  transfers between devices with their start and end apart: 5, of which 4 were waited for; matrix products, arithmetic and copies ran while one was open for 16% of the time, Pallas kernels for 0%

profile of v1, /device:TPU:0, one launch (start us, length us, event | category | flops | bytes accessed | tf_op | source)
XLA Modules:
  0.0 99.3 jit_solution(17368790370751411037)
XLA Ops:
  6.5 0.5 collective-permute-start
  7.0 0.5 broadcast.148
  7.5 1.3 %reduce.3 = s32[128]{0:T(128)S(1)} reduce(s32[128,1]{0,1:T(1,128)} %param.14, s32[]{:T(128)} %broadcast.148), dimensions={1}, to_apply=%param.14.reduce_sub_computation.3 | reduce | bytes 1028 | tf_op args[6]
  8.9 0.1 reshape_squeeze.3
  9.0 0.7 compare_convert_fusion
  9.7 0.7 sort.32
  10.4 0.1 copy.13
  10.5 0.1 reshape.126
  10.6 0.0 copy-start.2
  10.6 2.7 %gather_fusion.1 = bf16[32,128,128]{2,1,0:T(8,128)(2,1)} fusion(bf16[16,128,128]{2,1,0:T(8,128)(2,1)} %param.9, s32[1024]{0:T(1024)S(1)} %pad_clamp_fusion.2), kind=kCustom, calls=%fused_computation.1 | custom fusion | bytes 2097280 | tf_op jit(solution)/shard_map/gather | solution.py:52
  13.3 7.0 %all-to-all-start = ((bf16[8,4,128,128]{3,2,1,0:T(8,128)(2,1)}), bf16[8,4,128,128]{3,2,1,0:T(8,128)(2,1)}, u32[]{:S(2)}, u32[]{:S(2)}) async-start(bf16[8,4,128,128]{3,2,1,0:T(8,128)(2,1)} %bitcast.5), calls=%async_computation | async-start | bytes 2097152 | tf_op jit(solution)/shard_map/all_to_all | solution.py:53
  20.3 0.0 reduce-scatter.2.cloned.1.call-start
  20.3 0.6 dynamic_slice.10
  20.9 0.6 compare_convert_fusion.1
  21.6 0.1 copy.11
  21.6 0.7 sort.31
  22.4 0.1 copy.14
  22.4 0.1 reshape.164
  22.5 0.7 gather_fusion.6
  23.2 0.1 reshape.167
  23.3 0.1 copy.15
  23.4 1.4 %collective-permute-start.1 = (bf16[2048,128]{1,0:T(8,128)(2,1)S(1)}, bf16[2048,128]{1,0:T(8,128)(2,1)S(1)}, u32[]{:S(2)}, u32[]{:S(2)}) collective-permute-start(bf16[2048,128]{1,0:T(8,128)(2,1)S(1)} %collective-permute-done), channel_id=1, source_target_pairs={{0,8},{8,16},{16,24},{24,0},{1,9},{9,17},{17,25},{25,1},{2,10},{10... | collective-permute-start | bytes 1572872 | tf_op jit(solution)/shard_map/ppermute | solution.py:40
  24.7 0.1 copy.12
  24.8 0.1 reshape.112
  24.9 0.7 gather_fusion.2
  25.6 0.7 gather_fusion.4
  26.3 5.7 %collective-permute-done.1 = bf16[2048,128]{1,0:T(8,128)(2,1)S(1)} collective-permute-done((bf16[2048,128]{1,0:T(8,128)(2,1)S(1)}, bf16[2048,128]{1,0:T(8,128)(2,1)S(1)}, u32[]{:S(2)}, u32[]{:S(2)}) %collective-permute-start.1) | collective-permute-done | bytes 524320 | tf_op jit(solution)/shard_map/ppermute | solution.py:40
  32.0 0.1 copy.16
  32.1 0.1 convert_element_type.29
  32.2 0.7 gather_fusion
  32.9 1.7 %gather_fusion.5 = bf16[32,128,128]{2,1,0:T(8,128)(2,1)} fusion(bf16[26,128,128]{2,1,0:T(8,128)(2,1)S(1)} %copy-done, s32[1024]{0:T(1024)S(1)} %pad_clamp_fusion), kind=kCustom, calls=%fused_computation.5 | custom fusion | bytes 2097280 | tf_op jit(solution)/shard_map/gather | solution.py:17
  34.6 6.0 %collective-permute-done.2 = bf16[2048,128]{1,0:T(8,128)(2,1)S(1)} collective-permute-done((bf16[2048,128]{1,0:T(8,128)(2,1)S(1)}, bf16[2048,128]{1,0:T(8,128)(2,1)S(1)}, u32[]{:S(2)}, u32[]{:S(2)}) %collective-permute-start.2) | collective-permute-done | bytes 524320 | tf_op jit(solution)/shard_map/ppermute | solution.py:40
  40.7 0.1 constant_dynamic-update-slice_fusion.6
  40.7 0.1 constant_dynamic-update-slice_fusion.5
  40.8 0.1 constant_dynamic-update-slice_fusion.4
  40.9 0.1 constant_dynamic-update-slice_fusion.3
  41.0 0.1 constant_dynamic-update-slice_fusion.2
  41.1 0.1 constant_dynamic-update-slice_fusion.1
  41.1 0.1 constant_dynamic-update-slice_fusion
  41.2 0.1 constant_dynamic-slice_fusion
  41.4 1.7 %gather_fusion.3 = bf16[32,128,128]{2,1,0:T(8,128)(2,1)} fusion(bf16[64,128,128]{2,1,0:T(8,128)(2,1)S(1)} %bitcast.30, s32[1024]{0:T(1024)S(1)} %pad_clamp_fusion.1), kind=kCustom, calls=%fused_computation.3 | custom fusion | bytes 2097280 | tf_op jit(solution)/shard_map/gather | solution.py:12
  43.0 4.6 %all-to-all-done = bf16[8,4,128,128]{3,2,1,0:T(8,128)(2,1)} async-done(((bf16[8,4,128,128]{3,2,1,0:T(8,128)(2,1)}), bf16[8,4,128,128]{3,2,1,0:T(8,128)(2,1)}, u32[]{:S(2)}, u32[]{:S(2)}) %all-to-all-start) | async-done | bytes 1048608 | tf_op jit(solution)/shard_map/all_to_all | solution.py:53
  47.6 2.6 %convolution_multiply_fusion = f32[32,128,128]{2,1,0:T(8,128)S(1)} fusion(bf16[32,128,128]{2,1,0:T(8,128)(2,1)} %gather_fusion.5, bf16[32,128,128]{2,1,0:T(8,128)(2,1)} %bitcast.6, bf16[32,128,128]{2,1,0:T(8,128)(2,1)} %gather_fusion.3, f32[32]{0:T(128)S(1)} %convert_element_type.29), kind=kOutput, calls=%fused_computation.8 | convolution fusion | flops 269484032 | bytes 5243008 | tf_op jit(solution)/shard_map/kac,kcd->kad/dot_general | solution.py:16
  50.2 2.4 %broadcast_in_dim.8 = f32[64,128,128]{2,1,0:T(8,128)} broadcast(f32[]{:T(128)} %constant.27.clone.1), dimensions={} | broadcast | bytes 4194308 | tf_op jit(solution)/shard_map/broadcast_in_dim | solution.py:46
  52.6 6.1 %scatter_fusion = f32[64,128,128]{2,1,0:T(8,128)} fusion(f32[64,128,128]{2,1,0:T(8,128)} %broadcast_in_dim.8, s32[32]{0:T(128)S(1)} %fusion.1, f32[32,128,128]{2,1,0:T(8,128)S(1)} %convolution_multiply_fusion), kind=kCustom, calls=%fused_computation.7 | custom fusion | flops 524288 | bytes 6291584 | tf_op jit(solution)/shard_map/scatter-add | solution.py:20
  58.7 3.9 %convert_element_type.30 = bf16[64,128,128]{2,1,0:T(8,128)(2,1)} convert(f32[64,128,128]{2,1,0:T(8,128)} %scatter_fusion) | non-fusion elementwise | flops 1048576 | bytes 6291456 | tf_op jit(solution)/shard_map/convert_element_type | solution.py:75
  62.6 0.0 reduce-scatter.2.cloned.1.call-update
  62.7 29.8 %reduce-scatter.2.cloned.1.call-done = bf16[2048,128]{1,0:T(8,128)(2,1)} async-done(((bf16[8192,128]{1,0:T(8,128)(2,1)}), bf16[2048,128]{1,0:T(8,128)(2,1)}) %reduce-scatter.2.cloned.1.call-update) | async-done | bytes 524304 | tf_op jit(solution)/shard_map/reduce_scatter | solution.py:74
  (28 shorter events, 0.1 us)
Async XLA Ops:
  6.5 26.4 %copy-start = (bf16[26,128,128]{2,1,0:T(8,128)(2,1)S(1)}, bf16[26,128,128]{2,1,0:T(8,128)(2,1)}, u32[]{:S(2)}) copy-start(bf16[26,128,128]{2,1,0:T(8,128)(2,1)} %param.10) | copy-start | bytes 2555908
  6.5 13.8 %copy-start.5 = (s32[8]{0:T(128)S(1)}, s32[8]{0:T(128)}, u32[]{:S(2)}) copy-start(s32[8]{0:T(128)} %param.15) | copy-start | bytes 100
  6.5 16.8 %collective-permute-start = (bf16[2048,128]{1,0:T(8,128)(2,1)}, bf16[2048,128]{1,0:T(8,128)(2,1)S(1)}, u32[]{:S(2)}, u32[]{:S(2)}) collective-permute-start(bf16[2048,128]{1,0:T(8,128)(2,1)} %param.8), channel_id=1, source_target_pairs={{0,8},{8,16},{16,24},{24,0},{1,9},{9,17},{17,25},{25,1},{2,10},{10... | collective-permute-start | bytes 1572872 | tf_op jit(solution)/shard_map/ppermute | solution.py:40
  10.6 14.3 %copy-start.1 = (s32[128]{0:T(128)S(1)}, s32[128]{0:T(128)}, u32[]{:S(2)}) copy-start(s32[128]{0:T(128)} %param.11) | copy-start | bytes 1540
  10.6 15.0 %copy-start.2 = (s32[128]{0:T(128)S(1)}, s32[128]{0:T(128)}, u32[]{:S(2)}) copy-start(s32[128]{0:T(128)} %param.13) | copy-start | bytes 1540
  13.3 18.9 %copy-start.3 = (s32[128]{0:T(128)S(1)}, s32[128]{0:T(128)}, u32[]{:S(2)}) copy-start(s32[128]{0:T(128)} %param.12) | copy-start | bytes 1540
  13.3 34.3 %all-to-all-start = ((bf16[8,4,128,128]{3,2,1,0:T(8,128)(2,1)}), bf16[8,4,128,128]{3,2,1,0:T(8,128)(2,1)}, u32[]{:S(2)}, u32[]{:S(2)}) async-start(bf16[8,4,128,128]{3,2,1,0:T(8,128)(2,1)} %bitcast.5), calls=%async_computation | async-start | bytes 2097152 | tf_op jit(solution)/shard_map/all_to_all | solution.py:53
  20.3 72.2 %reduce-scatter.2.cloned.1.call-start = ((), (), s32[]{:S(2)}) async-start(), calls=%async_computation.2 | async-start | bytes 2621440 | tf_op jit(solution)/shard_map/reduce_scatter | solution.py:74
  23.2 17.6 %copy-start.4 = (bf16[2048,128]{1,0:T(8,128)(2,1)S(1)}, bf16[2048,128]{1,0:T(8,128)(2,1)}, u32[]{:S(2)}) copy-start(bf16[2048,128]{1,0:T(8,128)(2,1)} %param.8) | copy-start | bytes 1572868
  23.4 8.6 %collective-permute-start.1 = (bf16[2048,128]{1,0:T(8,128)(2,1)S(1)}, bf16[2048,128]{1,0:T(8,128)(2,1)S(1)}, u32[]{:S(2)}, u32[]{:S(2)}) collective-permute-start(bf16[2048,128]{1,0:T(8,128)(2,1)S(1)} %collective-permute-done), channel_id=1, source_target_pairs={{0,8},{8,16},{16,24},{24,0},{1,9},{9,17},{17,25},{25,1},{2,10},{10... | collective-permute-start | bytes 1572872 | tf_op jit(solution)/shard_map/ppermute | solution.py:40
  32.0 8.6 %collective-permute-start.2 = (bf16[2048,128]{1,0:T(8,128)(2,1)S(1)}, bf16[2048,128]{1,0:T(8,128)(2,1)S(1)}, u32[]{:S(2)}, u32[]{:S(2)}) collective-permute-start(bf16[2048,128]{1,0:T(8,128)(2,1)S(1)} %collective-permute-done.1), channel_id=1, source_target_pairs={{0,8},{8,16},{16,24},{24,0},{1,9},{9,17},{17,25},{25,1},{2,10},{10... | collective-permute-start | bytes 1572872 | tf_op jit(solution)/shard_map/ppermute | solution.py:40
Sparse Core Ops, SparseCore 0:
  62.8 29.6 reduce-scatter.1
